TPU v7x, 512 devices: a whole 4x8x8 slice. The times are simulated.
512 devices in a mesh: grp: 16 (over z, core), dev: 32 (over y, x).
Axes of the slice: x: 4, y: 8, z: 8, core: 2. Of those that a mesh axis runs over, the one named last changes fastest.
Arguments:
- stored_tiles: float32 [512, 33, 128, 128], P(('grp', 'dev')), may hold values from -0.22097087 to 0.22097087, as said below
- tile_flags: int32 [512, 33], P(('grp', 'dev')), may hold values from 0 to 1, as said below
- orbitals: float32 [65536, 256], P(('grp', 'dev')), may hold values from -6 to 6
Outputs:
- product: float32 [65536, 256], P(('grp', 'dev'))
Inputs may be any that keep to these rules, and one draw needn't show every extreme that they name: tile_flags[p, s] is 1 at s = p mod 32, 0 for s below that, and 0 at s = 32 in the last 32 block rows. `stored_tiles`: the tile at slot p mod 32 of block row p is symmetric.
All inputs are finite; a program needn't handle non-finite values.
Results may differ from a plain program's by a relative error of at most 0.000075.
Values sent between devices are 32-bit elements; how exact they have to be, the bound alone decides.
A program may use at most 64 MiB of HBM per device.

v0:
```python
import jax
import jax.numpy as jnp
from jax import lax
from jax.sharding import PartitionSpec as P


def shifted(shard, axis, by):
    count = lax.axis_size(axis)
    pairs = [(i, i + by) for i in range(count) if 0 <= i + by < count]
    return lax.ppermute(shard, axis, pairs)


def per_device(stored_tiles, tile_flags, orbitals):
    highest = lax.Precision.HIGHEST
    group_width = lax.axis_size("dev")
    own_index = lax.axis_index("dev")
    tile_order = stored_tiles.shape[2]
    columns = orbitals.shape[1]
    slot_index = lax.broadcasted_iota(jnp.int32, (group_width,), 0)
    flags_float = tile_flags[0].astype(jnp.float32)
    blocks = stored_tiles[0] * flags_float[:, None, None]
    in_group = blocks[:group_width]
    next_tile = blocks[group_width]
    beside = in_group * (slot_index != own_index).astype(jnp.float32)[:, None, None]
    piece_rows = lax.all_gather(orbitals, "dev", axis=0, tiled=True)
    num_slots = piece_rows.shape[0] // tile_order
    x_rows = piece_rows.reshape(num_slots, tile_order, columns)
    product = jnp.einsum("sij,sjk->ik", in_group, x_rows, precision=highest)
    row_count = lax.axis_size("dev") * orbitals.shape[0]
    terms = jnp.einsum("sji,jk->sik", beside, orbitals, precision=highest)
    product = product + lax.psum_scatter(
        terms.reshape(row_count, columns), "dev", scatter_dimension=0, tiled=True
    )
    following = shifted(orbitals, "grp", -1)
    product = product + jnp.dot(next_tile, following, precision=highest)
    upward = jnp.einsum("ji,jk->ik", next_tile, orbitals, precision=highest)
    product = product + shifted(upward, "grp", 1)
    return product


def solution(mesh):
    in_specs = (
        P(("grp", "dev"), None, None, None),
        P(("grp", "dev"), None),
        P(("grp", "dev"), None),
    )
    out_specs = P(("grp", "dev"), None)
    return jax.shard_map(
        per_device, mesh=mesh, in_specs=in_specs, out_specs=out_specs, check_vma=False
    )
```

profile of v0, /device:TPU:16, one launch (start us, length us, event | category | flops | bytes accessed | tf_op | source)
XLA Modules:
  0.0 342.0 jit_solution(7017481486420995727)
XLA Ops:
  6.5 0.0 all-gather.2.cloned.1.call-start
  6.5 0.7 all-gather.2.cloned.1.call-update
  7.3 0.0 reduce-scatter.2.cloned.1.call-start
  7.3 0.7 convert_bitcast_fusion
  8.0 0.0 copy-start
  8.0 1.8 bitcast_multiply_fusion
  9.8 0.0 copy-done
  9.8 5.7 %fusion = f32[32,128,256]{2,1,0:T(8,128)} fusion(f32[33,128,128]{2,1,0:T(8,128)S(1)} %bitcast_multiply_fusion, f32[32]{0:T(128)S(1)} %compare_convert_fusion, f32[128,256]{1,0:T(8,128)S(1)} %copy-done), kind=kOutput, calls=%fused_computation.2 | convolution fusion | flops 1611137024 | bytes 6423040 | tf_op jit(solution)/shard_map/sji,jk->sik/dot_general | solution.py:30
  15.5 0.0 reduce-scatter.2.cloned.1.call-update
  15.6 1.3 collective-permute-start
  16.9 0.3 fusion.5
  17.2 3.0 collective-permute-start.1
  20.2 80.8 %all-gather.2.cloned.1.call-done = f32[4096,256]{1,0:T(8,128)} async-done(((f32[128,256]{1,0:T(8,128)}), f32[4096,256]{1,0:T(8,128)}) %all-gather.2.cloned.1.call-update) | async-done | bytes 4194320 | tf_op jit(solution)/shard_map/all_gather | solution.py:25
  101.0 229.2 %reduce-scatter.2.cloned.1.call-done = f32[128,256]{1,0:T(8,128)} async-done(((f32[4096,256]{1,0:T(8,128)}), f32[128,256]{1,0:T(8,128)}) %reduce-scatter.2.cloned.1.call-update) | async-done | bytes 131088 | tf_op jit(solution)/shard_map/reduce_scatter | solution.py:31
  330.2 3.9 %fusion.2 = f32[128,256]{1,0:T(8,128)S(1)} fusion(f32[128,256]{1,0:T(8,128)} %reduce-scatter.2.cloned.1.call-done, f32[33,128,128]{2,1,0:T(8,128)S(1)} %bitcast_multiply_fusion, f32[32,128,256]{2,1,0:T(8,128)} %bitcast.22), kind=kOutput, calls=%fused_computation.6 | convolution fusion | flops 1610645504 | bytes 6619136 | tf_op jit(solution)/shard_map/sij,sjk->ik/dot_general | solution.py:28
  334.2 0.0 collective-permute-done.1
  334.2 0.0 collective-permute-done
  334.2 0.9 fusion.1
  (1 shorter events, 0.0 us)
Async XLA Ops:
  6.5 94.5 %all-gather.2.cloned.1.call-start = ((), (), s32[]{:S(2)}) async-start(), calls=%async_computation.1 | async-start | bytes 4325376 | tf_op jit(solution)/shard_map/all_gather | solution.py:25
  7.3 323.0 %reduce-scatter.2.cloned.1.call-start = ((), (), s32[]{:S(2)}) async-start(), calls=%async_computation.2 | async-start | bytes 4325376 | tf_op jit(solution)/shard_map/reduce_scatter | solution.py:31
  8.0 1.9 copy-start
  15.6 318.6 %collective-permute-start = (f32[128,256]{1,0:T(8,128)S(1)}, f32[128,256]{1,0:T(8,128)S(1)}, u32[]{:S(2)}, u32[]{:S(2)}) collective-permute-start(f32[128,256]{1,0:T(8,128)S(1)} %copy-done), channel_id=1, source_target_pairs={{32,0},{64,32},{96,64},{128,96},{160,128},{192,160},{224,192},{256... | collective-permute-start | bytes 393224 | tf_op jit(solution)/shard_map/ppermute | solution.py:10
  17.2 317.0 %collective-permute-start.1 = (f32[128,256]{1,0:T(8,128)S(1)}, f32[128,256]{1,0:T(8,128)S(1)}, u32[]{:S(2)}, u32[]{:S(2)}) collective-permute-start(f32[128,256]{1,0:T(8,128)S(1)} %fusion.5), channel_id=1, source_target_pairs={{0,32},{32,64},{64,96},{96,128},{128,160},{160,192},{192,224},{224... | collective-permute-start | bytes 393224 | tf_op jit(solution)/shard_map/ppermute | solution.py:10
Sparse Core Ops, SparseCore 0:
  10.5 90.4 all-gather.1
  105.5 224.7 reduce-scatter.1
where the time goes:
time: 342 us
  waiting for transfers between devices  311 us (91%)
  between operations  13.5 us (4%)
  matrix products  10.9 us (3%)
  starting transfers between devices  4.37 us (1%)
    reduce_scatter x1, waiting for transfers between devices, per_device(): lax.psum_scatter(terms.reshape(row_count, columns), 'dev', scatter_dimens...  229 us
    all_gather x1, waiting for transfers between devices, per_device(): piece_rows = lax.all_gather(orbitals, 'dev', axis=0, tiled=True)  80.8 us
  transfers between devices with their start and end apart: 4, of which 2 were waited for; matrix products, arithmetic and copies ran while one was open for 4% of the time, Pallas kernels for 0%

commit v1 on v0

--- a/solution.py
+++ b/solution.py
@@ -2,6 +2,11 @@
 import jax.numpy as jnp
 from jax import lax
 from jax.sharding import PartitionSpec as P
+
+
+def exchange_gather(x, axis, along):
+    outgoing = jnp.stack([x] * lax.axis_size(axis))
+    return jnp.concatenate(lax.all_to_all(outgoing, axis, 0, 0), axis=along)
 
 
 def shifted(shard, axis, by):
@@ -22,7 +27,7 @@
     in_group = blocks[:group_width]
     next_tile = blocks[group_width]
     beside = in_group * (slot_index != own_index).astype(jnp.float32)[:, None, None]
-    piece_rows = lax.all_gather(orbitals, "dev", axis=0, tiled=True)
+    piece_rows = exchange_gather(orbitals, "dev", 0)
     num_slots = piece_rows.shape[0] // tile_order
     x_rows = piece_rows.reshape(num_slots, tile_order, columns)
     product = jnp.einsum("sij,sjk->ik", in_group, x_rows, precision=highest)

time: 342 us -> 290 us (0.85)
  waiting for transfers between devices: 311 us -> 246 us
  starting transfers between devices: 4.37 us -> 14.5 us
    all_to_all x0 -> x1, waiting for transfers between devices: none -> 102 us  [exchange_gather(): return jnp.concatenate(lax.all_to_all(outgoing, axis, 0, 0), axis=along)]
    reduce_scatter x1, waiting for transfers between devices: 229 us -> 144 us  [per_device(): lax.psum_scatter(terms.reshape(row_count, columns), 'dev', scatter_dimens...]
    all_gather x1 -> x0, waiting for transfers between devices: 80.8 us -> none  [per_device(): piece_rows = lax.all_gather(orbitals, 'dev', axis=0, tiled=True)]
    all_to_all x0 -> x1, starting transfers between devices: none -> 10.2 us  [exchange_gather(): return jnp.concatenate(lax.all_to_all(outgoing, axis, 0, 0), axis=along)]
  transfers between devices with their start and end apart: 4 -> 4, of which waited for: 2 -> 2; matrix products, arithmetic and copies ran while one was open for 4% -> 2% of each run, Pallas kernels for 0% -> 0%
where the time goes in v1:
time: 290 us
  waiting for transfers between devices  246 us (85%)
  starting transfers between devices  14.5 us (5%)
  between operations  13.5 us (5%)
  matrix products  10.8 us (4%)
    reduce_scatter x1, waiting for transfers between devices, per_device(): lax.psum_scatter(terms.reshape(row_count, columns), 'dev', scatter_dimens...  144 us
    all_to_all x1, waiting for transfers between devices, exchange_gather(): return jnp.concatenate(lax.all_to_all(outgoing, axis, 0, 0), axis=along)  102 us
    all_to_all x1, starting transfers between devices, exchange_gather(): return jnp.concatenate(lax.all_to_all(outgoing, axis, 0, 0), axis=along)  10.2 us
  transfers between devices with their start and end apart: 4, of which 2 were waited for; matrix products, arithmetic and copies ran while one was open for 2% of the time, Pallas kernels for 0%

profile of v1, /device:TPU:16, one launch (start us, length us, event | category | flops | bytes accessed | tf_op | source)
XLA Modules:
  0.0 289.9 jit_solution(5337106617781189020)
XLA Ops:
  6.5 0.0 reduce-scatter.2.cloned.1.call-start
  6.5 0.7 convert_bitcast_fusion
  7.2 0.0 copy-start
  7.2 1.8 bitcast_multiply_fusion
  9.1 0.0 copy-done
  9.1 5.7 %fusion = f32[32,128,256]{2,1,0:T(8,128)} fusion(f32[33,128,128]{2,1,0:T(8,128)S(1)} %bitcast_multiply_fusion, f32[32]{0:T(128)S(1)} %compare_convert_fusion, f32[128,256]{1,0:T(8,128)S(1)} %copy-done), kind=kOutput, calls=%fused_computation.2 | convolution fusion | flops 1611137024 | bytes 6423040 | tf_op jit(solution)/shard_map/sji,jk->sik/dot_general | solution.py:35
  14.7 0.0 reduce-scatter.2.cloned.1.call-update
  14.7 2.4 stack.2
  17.2 10.2 %all-to-all-start = ((f32[32,128,256]{2,1,0:T(8,128)}), f32[32,128,256]{2,1,0:T(8,128)}, u32[]{:S(2)}, u32[]{:S(2)}) async-start(f32[32,128,256]{2,1,0:T(8,128)} %stack.2), calls=%async_computation | async-start | bytes 8388608 | tf_op jit(solution)/shard_map/all_to_all | solution.py:9
  27.4 1.3 collective-permute-start
  28.7 0.3 fusion.5
  29.0 3.0 %collective-permute-start.1 = (f32[128,256]{1,0:T(8,128)S(1)}, f32[128,256]{1,0:T(8,128)S(1)}, u32[]{:S(2)}, u32[]{:S(2)}) collective-permute-start(f32[128,256]{1,0:T(8,128)S(1)} %fusion.5), channel_id=1, source_target_pairs={{0,32},{32,64},{64,96},{96,128},{128,160},{160,192},{192,224},{224... | collective-permute-start | bytes 393224 | tf_op jit(solution)/shard_map/ppermute | solution.py:15
  32.0 102.3 %all-to-all-done = f32[32,128,256]{2,1,0:T(8,128)} async-done(((f32[32,128,256]{2,1,0:T(8,128)}), f32[32,128,256]{2,1,0:T(8,128)}, u32[]{:S(2)}, u32[]{:S(2)}) %all-to-all-start) | async-done | bytes 4194336 | tf_op jit(solution)/shard_map/all_to_all | solution.py:9
  134.3 143.9 %reduce-scatter.2.cloned.1.call-done = f32[128,256]{1,0:T(8,128)} async-done(((f32[4096,256]{1,0:T(8,128)}), f32[128,256]{1,0:T(8,128)}) %reduce-scatter.2.cloned.1.call-update) | async-done | bytes 131088 | tf_op jit(solution)/shard_map/reduce_scatter | solution.py:36
  278.2 3.9 %fusion.2 = f32[128,256]{1,0:T(8,128)S(1)} fusion(f32[128,256]{1,0:T(8,128)} %reduce-scatter.2.cloned.1.call-done, f32[33,128,128]{2,1,0:T(8,128)S(1)} %bitcast_multiply_fusion, f32[32,128,256]{2,1,0:T(8,128)} %all-to-all-done), kind=kOutput, calls=%fused_computation.6 | convolution fusion | flops 1610645504 | bytes 6619136 | tf_op jit(solution)/shard_map/sij,sjk->ik/dot_general | solution.py:33
  282.1 0.0 collective-permute-done.1
  282.1 0.0 collective-permute-done
  282.2 0.9 fusion.1
  (1 shorter events, 0.0 us)
Async XLA Ops:
  6.5 271.7 %reduce-scatter.2.cloned.1.call-start = ((), (), s32[]{:S(2)}) async-start(), calls=%async_computation.2 | async-start | bytes 4325376 | tf_op jit(solution)/shard_map/reduce_scatter | solution.py:36
  7.2 1.9 copy-start
  17.2 117.1 %all-to-all-start = ((f32[32,128,256]{2,1,0:T(8,128)}), f32[32,128,256]{2,1,0:T(8,128)}, u32[]{:S(2)}, u32[]{:S(2)}) async-start(f32[32,128,256]{2,1,0:T(8,128)} %stack.2), calls=%async_computation | async-start | bytes 8388608 | tf_op jit(solution)/shard_map/all_to_all | solution.py:9
  27.4 254.8 %collective-permute-start = (f32[128,256]{1,0:T(8,128)S(1)}, f32[128,256]{1,0:T(8,128)S(1)}, u32[]{:S(2)}, u32[]{:S(2)}) collective-permute-start(f32[128,256]{1,0:T(8,128)S(1)} %copy-done), channel_id=1, source_target_pairs={{32,0},{64,32},{96,64},{128,96},{160,128},{192,160},{224,192},{256... | collective-permute-start | bytes 393224 | tf_op jit(solution)/shard_map/ppermute | solution.py:15
  29.0 253.2 %collective-permute-start.1 = (f32[128,256]{1,0:T(8,128)S(1)}, f32[128,256]{1,0:T(8,128)S(1)}, u32[]{:S(2)}, u32[]{:S(2)}) collective-permute-start(f32[128,256]{1,0:T(8,128)S(1)} %fusion.5), channel_id=1, source_target_pairs={{0,32},{32,64},{64,96},{96,128},{128,160},{160,192},{192,224},{224... | collective-permute-start | bytes 393224 | tf_op jit(solution)/shard_map/ppermute | solution.py:15
Sparse Core Ops, SparseCore 0:
  14.9 263.2 reduce-scatter.1
